TPU v7x, 128 devices: a whole 4x4x4 slice. The times are simulated.
128 devices in a mesh: query: 4 (over z_lo, core), lib: 32 (over x, y, z_hi).
Axes of the slice: x: 4, y: 4, z: 4 (z_hi: 2, z_lo: 2; z = z_hi * 2 + z_lo), core: 2. Of those that a mesh axis runs over, the one named last changes fastest.
Arguments:
- queries: bfloat16 [4096, 2048], P(('query', 'lib')), may hold values from -64 to 64
- query_bucket: int32 [4096], P(('query', 'lib')), may hold values from 0 to 63, as said below
- library: bfloat16 [98304, 2048], P(('lib', 'query')), may hold values from -64 to 64
- library_time: bfloat16 [98304], P(('lib', 'query')), may hold values from 0 to 2
- library_bucket: int32 [98304], P(('lib', 'query')), may hold values from 0 to 63, as said below
Outputs:
- expected_spectra: bfloat16 [4096, 2048], P(('query', 'lib'))
- expected_time: float32 [4096], P(('query', 'lib'))
- log_evidence: float32 [4096], P(('query', 'lib'))
Inputs may be any that keep to these rules, and one draw needn't show every extreme that they name: `query_bucket`: library entries whose bucket differs from a query's by at most one are that query's candidates; the queries held by the devices at index i of lib lie in buckets 2 i and 2 i + 1. `library_bucket`: the library entries of every device hold each of the 64 buckets exactly 3072 // 256 times.
All inputs are finite; a program needn't handle non-finite values.
Results may differ from a plain program's by a relative error of at most 0.003.
Values may be sent and summed in bfloat16 or wider, within the bound.
A program may use at most 128 MiB of HBM per device.

v0:
```python
import jax
import jax.numpy as jnp
from jax import lax
from jax.sharding import PartitionSpec as P

SHARPNESS = 448
PER_BUCKET = 12
N_LIB = 32


def entry_scale(spectra_rows):
    return lax.rsqrt(jnp.mean(jnp.square(spectra_rows.astype(jnp.float32)), axis=1) + 1e-06)


def bucket_positions(bucket):
    n = bucket.shape[0]
    at = jnp.arange(n)
    same = (bucket[None, :] == bucket[:, None]) & (at[None, :] < at[:, None])
    rank = jnp.sum(same.astype(jnp.int32), axis=1)
    return bucket * PER_BUCKET + rank


def per_device(queries, query_bucket, library, library_time, library_bucket):
    own_rows, bin_count = queries.shape
    lib_at = lax.axis_index("lib")
    positions = bucket_positions(library_bucket)
    row = jnp.arange(N_LIB * 48)
    wanted = row // 48 * 24 - 12 + row % 48
    pick = (wanted[:, None] == positions[None, :]).astype(jnp.bfloat16)
    send = jnp.dot(pick, library, preferred_element_type=jnp.float32).astype(jnp.bfloat16)
    send_time = jnp.dot(pick, library_time, preferred_element_type=jnp.float32).astype(jnp.bfloat16)
    entries = lax.all_to_all(send.reshape(N_LIB, 48, bin_count), "lib", 0, 0).reshape(
        N_LIB * 48, bin_count
    )
    entry_time = lax.all_to_all(send_time.reshape(N_LIB, 48), "lib", 0, 0).reshape(N_LIB * 48)
    query_block = lax.all_gather(queries, "query", axis=0, tiled=True)
    block_bucket = lax.all_gather(query_bucket, "query", axis=0, tiled=True)
    query_scale = entry_scale(query_block) * (SHARPNESS / bin_count)
    products = lax.dot_general(
        query_block, entries, (((1,), (1,)), ((), ())), preferred_element_type=jnp.float32
    )
    row_bucket = 2 * lib_at - 1 + row % 48 // PER_BUCKET
    inside = jnp.abs(block_bucket[:, None] - row_bucket[None, :]) <= 1
    inside = inside & (row_bucket >= 0)[None, :] & (row_bucket < 2 * N_LIB)[None, :]
    scores = jnp.where(
        inside, products * query_scale[:, None] * entry_scale(entries)[None, :], -jnp.inf
    )
    maxima = lax.pmax(jnp.max(scores, axis=1), "query")
    weights = jnp.exp(scores - maxima[:, None]).astype(jnp.bfloat16)
    total_part = jnp.sum(weights.astype(jnp.float32), axis=1)
    spectra_part = jnp.dot(weights, entries, preferred_element_type=jnp.float32)
    time_part = jnp.dot(weights, entry_time, preferred_element_type=jnp.float32)
    total_all, time_all = lax.psum((total_part, time_part), "query")
    spectra_sum = lax.psum_scatter(spectra_part, "query", scatter_dimension=0, tiled=True)
    first_row = lax.axis_index("query") * own_rows
    totals = lax.dynamic_slice_in_dim(total_all, first_row, own_rows)
    time_sum = lax.dynamic_slice_in_dim(time_all, first_row, own_rows)
    own_maxima = lax.dynamic_slice_in_dim(maxima, first_row, own_rows)
    expected = (spectra_sum / totals[:, None]).astype(jnp.bfloat16)
    return (expected, time_sum / totals, own_maxima + jnp.log(totals))


def solution(mesh):
    placed = (
        P(("query", "lib"), None),
        P(("query", "lib")),
        P(("lib", "query"), None),
        P(("lib", "query")),
        P(("lib", "query")),
    )
    return jax.shard_map(
        per_device,
        mesh=mesh,
        in_specs=placed,
        out_specs=(P(("query", "lib"), None), P(("query", "lib")), P(("query", "lib"))),
        check_vma=False,
    )
```

profile of v0, /device:TPU:1, one launch (start us, length us, event | category | flops | bytes accessed | tf_op | source)
XLA Modules:
  0.0 188.5 jit_solution(15114478839216429072)
XLA Ops:
  7.2 0.0 copy-start
  7.2 1.2 convert_reduce_fusion
  8.4 0.7 multiply_add_fusion
  9.1 7.1 %convolution_convert_fusion = bf16[1536,2048]{1,0:T(8,128)(2,1)} fusion(bf16[768,2048]{1,0:T(8,128)(2,1)S(1)} %copy-done, s32[768]{0:T(1024)S(1)} %multiply_add_fusion, s32[1536]{0:T(1024)S(1)} %fusion.18), kind=kOutput, calls=%fused_computation.1 | convolution fusion | flops 4836163584 | bytes 9446400 | tf_op jit(solution)/shard_map/dot_general | solution.py:30
  16.2 11.4 %all-to-all-start = ((bf16[32,48,2048]{2,1,0:T(8,128)(2,1)}), bf16[32,48,2048]{2,1,0:T(8,128)(2,1)}, u32[]{:S(2)}, u32[]{:S(2)}) async-start(bf16[32,48,2048]{2,1,0:T(8,128)(2,1)} %bitcast.17), calls=%async_computation | async-start | bytes 12582912 | tf_op jit(solution)/shard_map/all_to_all | solution.py:32
  27.7 0.0 reduce-scatter.2.cloned.1.call-start
  27.7 0.6 dynamic-slice
  29.0 0.2 dynamic-update-slice
  29.2 24.7 %all-reduce = s32[128]{0:T(128)S(1)} all-reduce(s32[128]{0:T(128)S(1)} %dynamic-update-slice), channel_id=1, replica_groups=mesh['query'=4,'lib'=32] {'query'}, use_global_device_ids=true, to_apply=%add | all-reduce | flops 128 | bytes 1024
  54.0 17.4 %all_gather.7 = bf16[128,2048]{1,0:T(8,128)(2,1)S(1)} all-gather(bf16[32,2048]{1,0:T(8,128)(2,1)S(1)} %copy-done.2), channel_id=1, replica_groups=mesh['query'=4,'lib'=32] {'query'}, dimensions={0}, use_global_device_ids=true | all-gather | bytes 655360 | tf_op jit(solution)/shard_map/all_gather | solution.py:36
  71.4 0.8 copy-done.1
  72.2 0.2 multiply_reduce_fusion.1
  72.4 55.2 %all-to-all-done = bf16[32,48,2048]{2,1,0:T(8,128)(2,1)} async-done(((bf16[32,48,2048]{2,1,0:T(8,128)(2,1)}), bf16[32,48,2048]{2,1,0:T(8,128)(2,1)}, u32[]{:S(2)}, u32[]{:S(2)}) %all-to-all-start) | async-done | bytes 6291488 | tf_op jit(solution)/shard_map/all_to_all | solution.py:32
  127.6 4.1 %multiply_reduce_fusion = f32[32,48]{1,0:T(8,128)S(1)} fusion(bf16[32,48,2048]{2,1,0:T(8,128)(2,1)} %all-to-all-done), kind=kLoop, calls=%fused_computation | loop fusion | flops 9435648 | bytes 6297600 | tf_op jit(solution)/shard_map/reduce_sum | solution.py:12
  131.7 0.1 rsqrt.19
  131.7 5.0 %fusion.26 = (f32[128]{0:T(128)S(1)}, f32[128,1536]{0,1:T(8,128)}) fusion(f32[1536]{0:T(1024)S(1)} %rsqrt.19, f32[128]{0:T(128)S(1)} %rsqrt_multiply_fusion, bf16[1536,2048]{1,0:T(8,128)(2,1)} %bitcast.2, bf16[128,2048]{1,0:T(8,128)(2,1)} %copy-done.1, pred[1536]{0:T(1024)(128)(4,1)S(1)} %get-tuple-element.11, pred[1536]{0:T(1024)(128)(4,1)S(1)} %get-tuple-element.12, ...), kind=kOutput, calls=%fused_computation.50 | convolution fusion | flops 807075712 | bytes 7619072 | tf_op jit(solution)/shard_map/dot_general | solution.py:39
  136.7 8.2 %pmax.7 = f32[128]{0:T(128)S(1)} all-reduce(f32[128]{0:T(128)S(1)} %get-tuple-element.9), channel_id=1, replica_groups=mesh['query'=4,'lib'=32] {'query'}, use_global_device_ids=true, to_apply=%region_4.5 | all-reduce | flops 128 | bytes 1024 | tf_op jit(solution)/shard_map/pmax | solution.py:48
  144.9 1.9 convert_reduce_fusion.1
  146.8 4.8 %fusion.27 = f32[128,2048]{1,0:T(8,128)} fusion(bf16[128,1536]{0,1:T(8,128)(2,1)S(1)} %get-tuple-element.8, bf16[1536,2048]{1,0:T(8,128)(2,1)} %bitcast.2), kind=kOutput, calls=%fused_computation.51 | convolution fusion | flops 805306368 | bytes 7733248 | tf_op jit(solution)/shard_map/dot_general | solution.py:51
  151.6 0.0 reduce-scatter.2.cloned.1.call-update
  151.6 0.7 reshape.98
  152.3 0.9 fusion.11
  153.2 0.7 all_to_all.12
  153.9 6.9 %all-to-all-start.1 = ((bf16[32,1,48]{2,1,0:T(2,128)(2,1)}), bf16[32,1,48]{2,1,0:T(2,128)(2,1)S(1)}, u32[]{:S(2)}, u32[]{:S(2)}) async-start(bf16[32,1,48]{2,1,0:T(2,128)(2,1)} %all_to_all.12), calls=%async_computation.2 | async-start | bytes 32768 | tf_op jit(solution)/shard_map/all_to_all | solution.py:35
  160.8 8.5 %all-to-all-done.1 = bf16[32,1,48]{2,1,0:T(2,128)(2,1)S(1)} async-done(((bf16[32,1,48]{2,1,0:T(2,128)(2,1)}), bf16[32,1,48]{2,1,0:T(2,128)(2,1)S(1)}, u32[]{:S(2)}, u32[]{:S(2)}) %all-to-all-start.1) | async-done | bytes 3104 | tf_op jit(solution)/shard_map/all_to_all | solution.py:35
  169.3 0.7 reduce.2
  170.0 0.8 reshape.100
  170.8 0.2 convolution_bitcast_fusion
  170.9 7.2 %all-reduce.1 = (f32[128]{0:T(128)S(1)}, f32[128]{0:T(128)S(1)}) all-reduce(f32[128]{0:T(128)} %get-tuple-element.7, f32[128]{0:T(128)S(1)} %convolution_bitcast_fusion), channel_id=1, replica_groups=mesh['query'=4,'lib'=32] {'query'}, use_global_device_ids=true, to_apply=%region_7.8 | all-reduce | flops 256 | bytes 2048 | tf_op jit(solution)/shard_map/psum | solution.py:53
  178.1 1.3 log_add_fusion
  179.4 0.6 dynamic-slice_divide_fusion
  180.0 1.7 divide_convert_fusion
  (17 shorter events, 0.1 us)
Async XLA Ops:
  7.2 1.9 %copy-start = (bf16[768,2048]{1,0:T(8,128)(2,1)S(1)}, bf16[768,2048]{1,0:T(8,128)(2,1)}, u32[]{:S(2)}) copy-start(bf16[768,2048]{1,0:T(8,128)(2,1)} %param.7) | copy-start | bytes 9437188
  16.2 11.5 %copy-start.5 = (u32[128]{0:T(128)S(1)}, u32[128]{0:T(128)}, u32[]{:S(2)}) copy-start(u32[128]{0:T(128)} %constant.75) | copy-start | bytes 1540
  16.2 12.7 %copy-start.4 = (s32[32]{0:T(128)S(1)}, s32[32]{0:T(128)}, u32[]{:S(2)}) copy-start(s32[32]{0:T(128)} %param.6) | copy-start | bytes 388
  16.2 37.7 %copy-start.2 = (bf16[32,2048]{1,0:T(8,128)(2,1)S(1)}, bf16[32,2048]{1,0:T(8,128)(2,1)}, u32[]{:S(2)}) copy-start(bf16[32,2048]{1,0:T(8,128)(2,1)} %param.5) | copy-start | bytes 393220
  16.2 111.4 %all-to-all-start = ((bf16[32,48,2048]{2,1,0:T(8,128)(2,1)}), bf16[32,48,2048]{2,1,0:T(8,128)(2,1)}, u32[]{:S(2)}, u32[]{:S(2)}) async-start(bf16[32,48,2048]{2,1,0:T(8,128)(2,1)} %bitcast.17), calls=%async_computation | async-start | bytes 12582912 | tf_op jit(solution)/shard_map/all_to_all | solution.py:32
  27.7 152.3 %reduce-scatter.2.cloned.1.call-start = ((), (), s32[]{:S(2)}) async-start(), calls=%async_computation.3 | async-start | bytes 1310720 | tf_op jit(solution)/shard_map/reduce_scatter | solution.py:54
  71.4 0.8 copy-start.1
  144.9 6.7 %copy-start.3 = (f32[128]{0:T(128)}, f32[128]{0:T(128)S(1)}, u32[]{:S(2)}) copy-start(f32[128]{0:T(128)S(1)} %pmax.7) | copy-start | bytes 1540
  153.9 15.4 %all-to-all-start.1 = ((bf16[32,1,48]{2,1,0:T(2,128)(2,1)}), bf16[32,1,48]{2,1,0:T(2,128)(2,1)S(1)}, u32[]{:S(2)}, u32[]{:S(2)}) async-start(bf16[32,1,48]{2,1,0:T(2,128)(2,1)} %all_to_all.12), calls=%async_computation.2 | async-start | bytes 32768 | tf_op jit(solution)/shard_map/all_to_all | solution.py:35
Sparse Core Ops, SparseCore 0:
  151.8 19.7 reduce-scatter.1
where the time goes:
time: 189 us
  waiting for transfers between devices  63.8 us (34%)
  blocking collectives  57.5 us (30%)
  starting transfers between devices  18.3 us (10%)
  matrix products  18 us (10%)
  between operations  14.8 us (8%)
  other arithmetic  12.3 us (7%)
  local copies, waits for them, and re-layouts  3.92 us (2%)
    all_to_all x1, waiting for transfers between devices, per_device(): lax.all_to_all(send.reshape(N_LIB, 48, bin_count), 'lib', 0, 0)  55.2 us
    unnamed x1, blocking collectives  24.7 us
    all_gather x1, blocking collectives, per_device(): query_block = lax.all_gather(queries, 'query', axis=0, tiled=True)  17.4 us
    all_to_all x1, starting transfers between devices, per_device(): lax.all_to_all(send.reshape(N_LIB, 48, bin_count), 'lib', 0, 0)  11.4 us
    all_to_all x1, waiting for transfers between devices, per_device(): lax.all_to_all(send_time.reshape(N_LIB, 48), 'lib', 0, 0)  8.54 us
    pmax x1, blocking collectives, per_device(): maxima = lax.pmax(jnp.max(scores, axis=1), 'query')  8.21 us
    psum x1, blocking collectives, per_device(): total_all, time_all = lax.psum((total_part, time_part), 'query')  7.2 us
    dot_general x1, matrix products, per_device(): jnp.dot(pick, library, preferred_element_type=jnp.float32)  7.11 us
  transfers between devices with their start and end apart: 3, of which 2 were waited for; matrix products, arithmetic and copies ran while one was open for 3% of the time, Pallas kernels for 0%

commit v1 on v0

--- a/solution.py
+++ b/solution.py
@@ -33,7 +33,9 @@
         N_LIB * 48, bin_count
     )
     entry_time = lax.all_to_all(send_time.reshape(N_LIB, 48), "lib", 0, 0).reshape(N_LIB * 48)
-    query_block = lax.all_gather(queries, "query", axis=0, tiled=True)
+    query_block = jnp.concatenate(
+        lax.all_to_all(jnp.stack([queries] * lax.axis_size("query")), "query", 0, 0), axis=0
+    )
     block_bucket = lax.all_gather(query_bucket, "query", axis=0, tiled=True)
     query_scale = entry_scale(query_block) * (SHARPNESS / bin_count)
     products = lax.dot_general(

time: 189 us -> 202 us (1.069)
  waiting for transfers between devices: 63.8 us -> 87.4 us
  blocking collectives: 57.5 us -> 39.1 us
  starting transfers between devices: 18.3 us -> 23.7 us
    all_to_all x1, waiting for transfers between devices: 55.2 us -> 78.8 us  [per_device(): lax.all_to_all(send.reshape(N_LIB, 48, bin_count), 'lib', 0, 0)]
    all_gather x1 -> x0, blocking collectives: 17.4 us -> none  [per_device(): query_block = lax.all_gather(queries, 'query', axis=0, tiled=True)]
    all_to_all x0 -> x1, starting transfers between devices: none -> 5.48 us  [per_device(): lax.all_to_all(jnp.stack([queries] * lax.axis_size('query')), 'query', 0, 0)]
  transfers between devices with their start and end apart: 3 -> 4, of which waited for: 2 -> 2; matrix products, arithmetic and copies ran while one was open for 3% -> 8% of each run, Pallas kernels for 0% -> 0%
where the time goes in v1:
time: 202 us; the launch traced here: 201 us
  waiting for transfers between devices  87.4 us (43%)
  blocking collectives  39.1 us (19%)
  starting transfers between devices  23.7 us (12%)
  matrix products  17.9 us (9%)
  between operations  14.8 us (7%)
  other arithmetic  13.3 us (7%)
  local copies, waits for them, and re-layouts  5.07 us (3%)
    all_to_all x1, waiting for transfers between devices, per_device(): lax.all_to_all(send.reshape(N_LIB, 48, bin_count), 'lib', 0, 0)  78.8 us
    unnamed x1, blocking collectives  25 us
    all_to_all x1, starting transfers between devices, per_device(): lax.all_to_all(send.reshape(N_LIB, 48, bin_count), 'lib', 0, 0)  10.7 us
    all_to_all x1, waiting for transfers between devices, per_device(): lax.all_to_all(send_time.reshape(N_LIB, 48), 'lib', 0, 0)  8.54 us
    all_to_all x1, starting transfers between devices, per_device(): lax.all_to_all(send_time.reshape(N_LIB, 48), 'lib', 0, 0)  7.48 us
    psum x1, blocking collectives, per_device(): total_all, time_all = lax.psum((total_part, time_part), 'query')  7.2 us
    dot_general x1, matrix products, per_device(): jnp.dot(pick, library, preferred_element_type=jnp.float32)  7.11 us
    pmax x1, blocking collectives, per_device(): maxima = lax.pmax(jnp.max(scores, axis=1), 'query')  6.97 us
  transfers between devices with their start and end apart: 4, of which 2 were waited for; matrix products, arithmetic and copies ran while one was open for 8% of the time, Pallas kernels for 0%

profile of v1, /device:TPU:1, one launch (start us, length us, event | category | flops | bytes accessed | tf_op | source)
XLA Modules:
  0.0 201.3 jit_solution(13928245401760167857)
XLA Ops:
  7.2 1.9 stack.2
  9.1 5.5 %all-to-all-start.1 = ((bf16[4,32,2048]{2,1,0:T(8,128)(2,1)}), bf16[4,32,2048]{2,1,0:T(8,128)(2,1)}, u32[]{:S(2)}, u32[]{:S(2)}) async-start(bf16[4,32,2048]{2,1,0:T(8,128)(2,1)} %stack.2), calls=%async_computation.1 | async-start | bytes 1048576 | tf_op jit(solution)/shard_map/all_to_all | solution.py:37
  14.6 1.1 convert_reduce_fusion
  15.7 0.7 multiply_add_fusion
  16.4 7.1 %convolution_convert_fusion = bf16[1536,2048]{1,0:T(8,128)(2,1)} fusion(bf16[768,2048]{1,0:T(8,128)(2,1)S(1)} %copy-done, s32[768]{0:T(1024)S(1)} %multiply_add_fusion, s32[1536]{0:T(1024)S(1)} %fusion.18), kind=kOutput, calls=%fused_computation.1 | convolution fusion | flops 4836163584 | bytes 9446400 | tf_op jit(solution)/shard_map/dot_general | solution.py:30
  23.5 10.7 %all-to-all-start = ((bf16[32,48,2048]{2,1,0:T(8,128)(2,1)}), bf16[32,48,2048]{2,1,0:T(8,128)(2,1)}, u32[]{:S(2)}, u32[]{:S(2)}) async-start(bf16[32,48,2048]{2,1,0:T(8,128)(2,1)} %bitcast.18), calls=%async_computation | async-start | bytes 12582912 | tf_op jit(solution)/shard_map/all_to_all | solution.py:32
  34.2 0.0 reduce-scatter.2.cloned.1.call-start
  34.3 0.6 dynamic-slice
  35.6 0.2 dynamic-update-slice
  35.8 25.0 %all-reduce = s32[128]{0:T(128)S(1)} all-reduce(s32[128]{0:T(128)S(1)} %dynamic-update-slice), channel_id=1, replica_groups=mesh['query'=4,'lib'=32] {'query'}, use_global_device_ids=true, to_apply=%add | all-reduce | flops 128 | bytes 1024
  60.8 1.2 multiply_reduce_fusion.1
  62.1 0.1 mul.58
  62.1 78.8 %all-to-all-done = bf16[32,48,2048]{2,1,0:T(8,128)(2,1)} async-done(((bf16[32,48,2048]{2,1,0:T(8,128)(2,1)}), bf16[32,48,2048]{2,1,0:T(8,128)(2,1)}, u32[]{:S(2)}, u32[]{:S(2)}) %all-to-all-start) | async-done | bytes 6291488 | tf_op jit(solution)/shard_map/all_to_all | solution.py:32
  141.0 4.1 %multiply_reduce_fusion = f32[32,48]{1,0:T(8,128)S(1)} fusion(bf16[32,48,2048]{2,1,0:T(8,128)(2,1)} %all-to-all-done), kind=kLoop, calls=%fused_computation | loop fusion | flops 9435648 | bytes 6297600 | tf_op jit(solution)/shard_map/reduce_sum | solution.py:12
  145.1 0.1 rsqrt.20
  145.1 5.0 %fusion.26 = (f32[128]{0:T(128)S(1)}, f32[128,1536]{0,1:T(8,128)}) fusion(f32[1536]{0:T(1024)S(1)} %rsqrt.20, f32[128]{0:T(128)S(1)} %mul.58, bf16[1536,2048]{1,0:T(8,128)(2,1)} %bitcast.2, bf16[128,2048]{1,0:T(8,128)(2,1)} %bitcast.3, pred[1536]{0:T(1024)(128)(4,1)S(1)} %get-tuple-element.11, pred[1536]{0:T(1024)(128)(4,1)S(1)} %get-tuple-element.12, ...), kind=kOutput, calls=%fused_computation.50 | convolution fusion | flops 807075712 | bytes 7619072 | tf_op jit(solution)/shard_map/dot_general | solution.py:41
  150.1 7.0 %pmax.7 = f32[128]{0:T(128)S(1)} all-reduce(f32[128]{0:T(128)S(1)} %get-tuple-element.9), channel_id=1, replica_groups=mesh['query'=4,'lib'=32] {'query'}, use_global_device_ids=true, to_apply=%region_4.5 | all-reduce | flops 128 | bytes 1024 | tf_op jit(solution)/shard_map/pmax | solution.py:50
  157.1 1.9 convert_reduce_fusion.1
  159.0 4.8 %fusion.27 = f32[128,2048]{1,0:T(8,128)} fusion(bf16[128,1536]{0,1:T(8,128)(2,1)S(1)} %get-tuple-element.8, bf16[1536,2048]{1,0:T(8,128)(2,1)} %bitcast.2), kind=kOutput, calls=%fused_computation.51 | convolution fusion | flops 805306368 | bytes 7733248 | tf_op jit(solution)/shard_map/dot_general | solution.py:53
  163.8 0.0 reduce-scatter.2.cloned.1.call-update
  163.8 0.7 reshape.115
  164.5 0.9 fusion.11
  165.4 0.7 all_to_all.16
  166.1 7.5 %all-to-all-start.2 = ((bf16[32,1,48]{2,1,0:T(2,128)(2,1)}), bf16[32,1,48]{2,1,0:T(2,128)(2,1)S(1)}, u32[]{:S(2)}, u32[]{:S(2)}) async-start(bf16[32,1,48]{2,1,0:T(2,128)(2,1)} %all_to_all.16), calls=%async_computation.3 | async-start | bytes 32768 | tf_op jit(solution)/shard_map/all_to_all | solution.py:35
  173.6 8.5 %all-to-all-done.2 = bf16[32,1,48]{2,1,0:T(2,128)(2,1)S(1)} async-done(((bf16[32,1,48]{2,1,0:T(2,128)(2,1)}), bf16[32,1,48]{2,1,0:T(2,128)(2,1)S(1)}, u32[]{:S(2)}, u32[]{:S(2)}) %all-to-all-start.2) | async-done | bytes 3104 | tf_op jit(solution)/shard_map/all_to_all | solution.py:35
  182.1 0.7 reduce.3
  182.8 0.8 reshape.117
  183.5 0.2 convolution_bitcast_fusion
  183.7 7.2 %all-reduce.1 = (f32[128]{0:T(128)S(1)}, f32[128]{0:T(128)S(1)}) all-reduce(f32[128]{0:T(128)} %get-tuple-element.7, f32[128]{0:T(128)S(1)} %convolution_bitcast_fusion), channel_id=1, replica_groups=mesh['query'=4,'lib'=32] {'query'}, use_global_device_ids=true, to_apply=%region_7.8 | all-reduce | flops 256 | bytes 2048 | tf_op jit(solution)/shard_map/psum | solution.py:55
  190.9 1.3 log_add_fusion
  192.2 0.6 dynamic-slice_divide_fusion
  192.8 1.7 divide_convert_fusion
  (16 shorter events, 0.1 us)
Async XLA Ops:
  7.2 9.2 %copy-start = (bf16[768,2048]{1,0:T(8,128)(2,1)S(1)}, bf16[768,2048]{1,0:T(8,128)(2,1)}, u32[]{:S(2)}) copy-start(bf16[768,2048]{1,0:T(8,128)(2,1)} %param.7) | copy-start | bytes 9437188
  9.1 14.4 %all-to-all-start.1 = ((bf16[4,32,2048]{2,1,0:T(8,128)(2,1)}), bf16[4,32,2048]{2,1,0:T(8,128)(2,1)}, u32[]{:S(2)}, u32[]{:S(2)}) async-start(bf16[4,32,2048]{2,1,0:T(8,128)(2,1)} %stack.2), calls=%async_computation.1 | async-start | bytes 1048576 | tf_op jit(solution)/shard_map/all_to_all | solution.py:37
  23.5 10.8 %copy-start.3 = (u32[128]{0:T(128)S(1)}, u32[128]{0:T(128)}, u32[]{:S(2)}) copy-start(u32[128]{0:T(128)} %constant.75) | copy-start | bytes 1540
  23.5 12.0 %copy-start.2 = (s32[32]{0:T(128)S(1)}, s32[32]{0:T(128)}, u32[]{:S(2)}) copy-start(s32[32]{0:T(128)} %param.6) | copy-start | bytes 388
  23.5 117.5 %all-to-all-start = ((bf16[32,48,2048]{2,1,0:T(8,128)(2,1)}), bf16[32,48,2048]{2,1,0:T(8,128)(2,1)}, u32[]{:S(2)}, u32[]{:S(2)}) async-start(bf16[32,48,2048]{2,1,0:T(8,128)(2,1)} %bitcast.18), calls=%async_computation | async-start | bytes 12582912 | tf_op jit(solution)/shard_map/all_to_all | solution.py:32
  34.2 158.5 %reduce-scatter.2.cloned.1.call-start = ((), (), s32[]{:S(2)}) async-start(), calls=%async_computation.4 | async-start | bytes 1310720 | tf_op jit(solution)/shard_map/reduce_scatter | solution.py:56
  157.1 6.7 %copy-start.1 = (f32[128]{0:T(128)}, f32[128]{0:T(128)S(1)}, u32[]{:S(2)}) copy-start(f32[128]{0:T(128)S(1)} %pmax.7) | copy-start | bytes 1540
  166.1 16.0 %all-to-all-start.2 = ((bf16[32,1,48]{2,1,0:T(2,128)(2,1)}), bf16[32,1,48]{2,1,0:T(2,128)(2,1)S(1)}, u32[]{:S(2)}, u32[]{:S(2)}) async-start(bf16[32,1,48]{2,1,0:T(2,128)(2,1)} %all_to_all.16), calls=%async_computation.3 | async-start | bytes 32768 | tf_op jit(solution)/shard_map/all_to_all | solution.py:35
Sparse Core Ops, SparseCore 0:
  163.9 20.2 reduce-scatter.1
